TPU v7x, 32 devices: a whole 2x2x4 slice. The times are simulated.
32 devices in a mesh: feat: 4 (over y, x), label: 8 (over z, core).
Axes of the slice: x: 2, y: 2, z: 4, core: 2. Of those that a mesh axis runs over, the one named last changes fastest.
Arguments:
- documents: bfloat16 [160, 1024], P(None, 'label'), may hold values from -6 to 6
- expand_weight: bfloat16 [1024, 32768], P('label', 'feat'), may hold values from -0.1875 to 0.1875
- sparse_weight: bfloat16 [768, 16, 128, 128], P(('feat', 'label')), may hold values from -0.125 to 0.125
- feature_lists: int32 [768, 16], replicated, may hold values from 0 to 255, as said below
- positives: int32 [160, 8], replicated, may hold values from 0 to 98303
Outputs:
- grad_expand: bfloat16 [1024, 32768], P('label', 'feat')
- grad_sparse: bfloat16 [768, 16, 128, 128], P(('feat', 'label'))
Inputs may be any that keep to these rules, and one draw needn't show every extreme that they name: `feature_lists`: within each aligned group of 24 label blocks (taken in order), the entries name exactly 24 distinct feature blocks from each range of 64 consecutive blocks, each named exactly 4 times in the group; the 16 entries of one label block are distinct.
All inputs are finite; a program needn't handle non-finite values.
Results may differ from a plain program's by a relative error of at most 0.014.
Values may be sent and summed in bfloat16 or wider, within the bound.
No kernel may reach another device: no remote copies, remote signals or barrier semaphores. Data moves between devices by JAX's collectives and lax.ppermute only.
A program may use at most 192 MiB of HBM per device.

v0:
```python
import jax
import jax.numpy as jnp
from jax import lax
from jax.sharding import PartitionSpec as P

BLK = 128
FBLOCKS = 256
SLOTS = 16
LBLK_DEV = 24
CAP = 24


def on_device(documents, expand_weight, sparse_weight, feature_lists, positives):
    feat_count = lax.axis_size("feat")
    label_count = lax.axis_size("label")
    feat_index = lax.axis_index("feat")
    label_index = lax.axis_index("label")
    group = feat_index * label_count + label_index
    doc_count = documents.shape[0]
    width_local = expand_weight.shape[0]
    own_count = expand_weight.shape[1] // BLK
    local_weight = expand_weight.reshape(width_local, own_count, BLK)
    partial_pre = jnp.einsum(
        "dk,kbc->bdc", documents, local_weight, preferred_element_type=jnp.float32
    )
    summed_pre = lax.psum(partial_pre, "label")
    hidden = jnp.maximum(summed_pre, 0.0).astype(jnp.bfloat16)
    mine = lax.dynamic_slice_in_dim(feature_lists, group * LBLK_DEV, LBLK_DEV, 0)

    def sender_list(target):
        rows = lax.dynamic_slice_in_dim(
            feature_lists, (target * label_count + label_index) * LBLK_DEV, LBLK_DEV, 0
        )
        local_ids = feat_index * own_count + jnp.arange(own_count, dtype=jnp.int32)
        used = jnp.any(rows.reshape(-1)[:, None] == local_ids[None, :], axis=0)
        order = jnp.argsort(jnp.where(used, 0, 1).astype(jnp.int32), stable=True)
        return order[:CAP]

    send_index = jax.vmap(sender_list)(jnp.arange(feat_count, dtype=jnp.int32))
    outgoing = jnp.take(hidden, send_index, axis=0)
    incoming = lax.all_to_all(outgoing, "feat", split_axis=0, concat_axis=0, tiled=True)
    present = jnp.any(
        mine.reshape(-1)[:, None] == jnp.arange(FBLOCKS, dtype=jnp.int32)[None, :], axis=0
    )
    ranks = jnp.cumsum(present.reshape(feat_count, own_count).astype(jnp.int32), axis=1) - 1
    position_table = (jnp.arange(feat_count, dtype=jnp.int32)[:, None] * CAP + ranks).reshape(-1)
    slot_position = jnp.take(position_table, mine, axis=0)
    picked = jnp.take(incoming.reshape(feat_count * CAP, doc_count, BLK), slot_position, axis=0)
    logits = jnp.einsum("lsdc,lsce->dle", picked, sparse_weight, preferred_element_type=jnp.float32)
    label_ids = (group * LBLK_DEV + jnp.arange(LBLK_DEV, dtype=jnp.int32))[
        :, None
    ] * BLK + jnp.arange(BLK, dtype=jnp.int32)[None, :]
    targets = jnp.any(positives[:, :, None, None] == label_ids[None, None, :, :], axis=1).astype(
        jnp.float32
    )
    residual = (jax.nn.sigmoid(logits) - targets).astype(jnp.bfloat16)
    grad_sparse = jnp.einsum(
        "lsdc,dle->lsce", picked, residual, preferred_element_type=jnp.float32
    ).astype(jnp.bfloat16)
    back = jnp.einsum("dle,lsce->lsdc", residual, sparse_weight, preferred_element_type=jnp.float32)
    back_rows = back.reshape(LBLK_DEV * SLOTS, doc_count, BLK)
    group_part = jax.ops.segment_sum(
        back_rows, slot_position.reshape(-1), num_segments=feat_count * CAP
    )
    group_part = group_part.astype(jnp.bfloat16).reshape(feat_count, CAP, doc_count, BLK)
    returned = lax.all_to_all(group_part, "feat", split_axis=0, concat_axis=0, tiled=True)
    column_sum = jax.ops.segment_sum(
        returned.astype(jnp.float32).reshape(feat_count * CAP, doc_count, BLK),
        send_index.reshape(-1),
        num_segments=own_count,
    )
    block_grad = lax.psum(column_sum.astype(jnp.bfloat16), "label").astype(jnp.float32)
    grad_hidden = jnp.where(hidden > 0, block_grad, 0.0).astype(jnp.bfloat16)
    grad_expand = jnp.einsum(
        "dk,bdc->kbc", documents, grad_hidden, preferred_element_type=jnp.float32
    )
    grad_expand = grad_expand.reshape(width_local, own_count * BLK).astype(jnp.bfloat16)
    return (grad_expand, grad_sparse)


def solution(mesh):
    return jax.shard_map(
        on_device,
        mesh=mesh,
        in_specs=(
            P(None, "label"),
            P("label", "feat"),
            P(("feat", "label"), None, None, None),
            P(),
            P(),
        ),
        out_specs=(P("label", "feat"), P(("feat", "label"), None, None, None)),
        check_vma=False,
    )
```

profile of v0, /device:TPU:0, one launch (start us, length us, event | category | flops | bytes accessed | tf_op | source)
XLA Modules:
  0.0 502.6 jit_solution(14127657274373574968)
XLA Ops:
  7.2 8.1 %while.1 = (s32[]{:T(128)}, s32[768,16]{0,1:T(8,128)}, s32[4,2]{0,1:T(2,128)S(1)}, s32[4,24,16]{1,2,0:T(8,128)S(1)}, s32[]{:T(128)}) while((s32[]{:T(128)}, s32[768,16]{0,1:T(8,128)}, s32[4,2]{0,1:T(2,128)S(1)}, s32[4,24,16]{1,2,0:T(8,128)S(1)}, s32[]{:T(128)}) %tuple.25), condition=%wide.while_cond, body=%wide.while_body.sunk | while | flops 2 | bytes 9825 | solution.py:31
  17.1 4.0 convolution_bitcast_fusion
  21.1 111.1 %all-reduce.5 = bf16[64,160,128]{2,1,0:T(8,128)(2,1)} all-reduce(f32[64,160,128]{2,1,0:T(8,128)} %convolution_bitcast_fusion), channel_id=1, replica_groups=mesh['feat'=4,'label'=8] {'label'}, use_global_device_ids=true, to_apply=%region_0.0 | all-reduce | flops 1310720 | bytes 7864320 | tf_op jit(solution)/shard_map/psum | solution.py:26
  132.1 3.8 maximum_convert_fusion
  136.0 4.8 gather_fusion.1
  140.8 4.5 broadcast_select_fusion.5
  145.3 5.0 all-to-all-start
  155.3 3.7 compare_reduce_fusion
  159.0 32.3 %all-to-all-done = bf16[4,24,160,128]{3,2,1,0:T(8,128)(2,1)} async-done(((bf16[4,24,160,128]{3,2,1,0:T(8,128)(2,1)}), bf16[4,24,160,128]{3,2,1,0:T(8,128)(2,1)}, u32[]{:S(2)}, u32[]{:S(2)}) %all-to-all-start) | async-done | bytes 3932192 | tf_op jit(solution)/shard_map/all_to_all | solution.py:41
  191.3 14.7 %gather_fusion.2 = bf16[384,160,128]{2,1,0:T(8,128)(2,1)} fusion(bf16[96,160,128]{2,1,0:T(8,128)(2,1)} %bitcast.3, s32[1024]{0:T(1024)S(1)} %pad_clamp_fusion), kind=kCustom, calls=%fused_computation.2 | custom fusion | bytes 31458816 | tf_op jit(solution)/shard_map/jit(_take)/gather | solution.py:48
  206.0 11.4 %fusion.14 = bf16[160,24,128,1]{2,0,3,1:T(8,128)(2,1)S(1)} fusion(pred[160,24,128]{2,1,0:T(8,128)(4,1)S(1)} %compare_reduce_fusion, bf16[24,16,128,128]{3,2,1,0:T(8,128)(2,1)} %param.7, bf16[24,16,160,128]{3,2,1,0:T(8,128)(2,1)} %bitcast.62, pred[24,16]{1,0:T(8,128)(4,1)S(1)} %get-tuple-element.26), kind=kOutput, calls=%fused_computation.30 | convolution fusion | flops 2024079360 | bytes 29786496 | tf_op jit(solution)/shard_map/lsdc,lsce->dle/dot_general | solution.py:49
  217.4 15.2 %fusion.23 = f32[24,160,16,128]{3,1,2,0:T(8,128)} fusion(bf16[160,24,128,1]{2,0,3,1:T(8,128)(2,1)S(1)} %fusion.14, bf16[24,16,128,128]{3,2,1,0:T(8,128)(2,1)} %param.7), kind=kOutput, calls=%fused_computation.58 | convolution fusion | flops 2013265920 | bytes 45023232 | tf_op jit(solution)/shard_map/dle,lsce->lsdc/dot_general | solution.py:60
  232.6 4.2 broadcast_in_dim.58
  236.8 87.4 %scatter_fusion = f32[96,160,128]{2,1,0:T(8,128)} fusion(f32[96,160,128]{2,1,0:T(8,128)} %broadcast_in_dim.58, s32[384]{0:T(512)S(1)} %reshape.186, f32[384,160,128]{2,1,0:T(8,128)} %bitcast.61), kind=kCustom, calls=%fused_computation.3 | custom fusion | flops 7864320 | bytes 94373376 | tf_op jit(solution)/shard_map/scatter-add | solution.py:62
  324.3 5.8 %convert_element_type.45 = bf16[96,160,128]{2,1,0:T(8,128)(2,1)} convert(f32[96,160,128]{2,1,0:T(8,128)} %scatter_fusion) | non-fusion elementwise | flops 1966080 | bytes 11796480 | tf_op jit(solution)/shard_map/convert_element_type | solution.py:65
  330.1 4.8 all-to-all-start.1
  335.4 43.7 %all-to-all-done.1 = bf16[4,24,160,128]{3,2,1,0:T(8,128)(2,1)} async-done(((bf16[4,24,160,128]{3,2,1,0:T(8,128)(2,1)}), bf16[4,24,160,128]{3,2,1,0:T(8,128)(2,1)}, u32[]{:S(2)}, u32[]{:S(2)}) %all-to-all-start.1) | async-done | bytes 3932192 | tf_op jit(solution)/shard_map/all_to_all | solution.py:66
  379.1 6.4 %bitcast_convert_fusion = f32[96,160,128]{2,1,0:T(8,128)} fusion(bf16[4,24,160,128]{3,2,1,0:T(8,128)(2,1)} %all-to-all-done.1), kind=kLoop, calls=%fused_computation.16 | loop fusion | flops 1966080 | bytes 11796480 | tf_op jit(solution)/shard_map/reshape | solution.py:68
  388.4 22.5 %scatter_fusion.1 = f32[64,160,128]{2,1,0:T(8,128)} fusion(f32[64,160,128]{2,1,0:T(8,128)} %broadcast.134, s32[96]{0:T(128)S(1)} %reshape.194, f32[96,160,128]{2,1,0:T(8,128)} %bitcast_convert_fusion), kind=kCustom, calls=%fused_computation.4 | custom fusion | flops 1966080 | bytes 23593344 | tf_op jit(solution)/shard_map/scatter-add | solution.py:67
  411.0 4.4 convert_element_type.46
  415.4 14.3 %fusion.4 = bf16[24,16,128,128]{3,2,1,0:T(8,128)(2,1)} fusion(bf16[160,24,128,1]{2,0,3,1:T(8,128)(2,1)S(1)} %fusion.14, bf16[24,16,160,128]{3,2,1,0:T(8,128)(2,1)} %bitcast.63, pred[24,16]{1,0:T(8,128)(4,1)S(1)} %get-tuple-element.26), kind=kOutput, calls=%fused_computation.13 | convolution fusion | flops 2027421696 | bytes 29294976 | tf_op jit(solution)/shard_map/lsdc,dle->lsce/dot_general | solution.py:57
  429.6 56.8 %all-reduce.4.cloned.1.call-done = bf16[64,160,128]{2,1,0:T(8,128)(2,1)} async-done(((bf16[64,160,128]{2,1,0:T(8,128)(2,1)}), bf16[64,160,128]{2,1,0:T(8,128)(2,1)}) %all-reduce.4.cloned.1.call-update) | async-done | bytes 2621456 | tf_op jit(solution)/shard_map/psum | solution.py:72
  486.5 5.2 %fusion.13 = bf16[64,128,128]{2,1,0:T(8,128)(2,1)} fusion(bf16[64,160,128]{2,1,0:T(8,128)(2,1)} %all-reduce.4.cloned.1.call-done, bf16[160,128]{1,0:T(8,128)(2,1)S(1)} %copy-done.2, bf16[64,160,128]{2,1,0:T(8,128)(2,1)} %all-reduce.5), kind=kOutput, calls=%fused_computation.29 | convolution fusion | flops 345767936 | bytes 7380992 | tf_op jit(solution)/shard_map/dk,bdc->kbc/dot_general | solution.py:74
  491.6 4.1 copy.28
  (65 shorter events, 18.3 us)
Async XLA Ops:
  7.2 9.9 %copy-start = (bf16[128,8192]{1,0:T(8,128)(2,1)S(1)}, bf16[128,8192]{1,0:T(8,128)(2,1)}, u32[]{:S(2)}) copy-start(bf16[128,8192]{1,0:T(8,128)(2,1)} %param.6) | copy-start | bytes 6291460
  145.3 46.0 %all-to-all-start = ((bf16[4,24,160,128]{3,2,1,0:T(8,128)(2,1)}), bf16[4,24,160,128]{3,2,1,0:T(8,128)(2,1)}, u32[]{:S(2)}, u32[]{:S(2)}) async-start(bf16[4,24,160,128]{3,2,1,0:T(8,128)(2,1)} %broadcast_select_fusion.5), calls=%async_computation | async-start | bytes 7864320 | tf_op jit(solution)/shard_map/all_to_all | solution.py:41
  152.0 3.1 copy-start.3
  330.1 48.9 %all-to-all-start.1 = ((bf16[4,24,160,128]{3,2,1,0:T(8,128)(2,1)}), bf16[4,24,160,128]{3,2,1,0:T(8,128)(2,1)}, u32[]{:S(2)}, u32[]{:S(2)}) async-start(bf16[4,24,160,128]{3,2,1,0:T(8,128)(2,1)} %bitcast.64), calls=%async_computation.1 | async-start | bytes 7864320 | tf_op jit(solution)/shard_map/all_to_all | solution.py:66
  334.9 151.5 %all-reduce.4.cloned.1.call-start = ((), (), s32[]{:S(2)}) async-start(), calls=%async_computation.2 | async-start | bytes 5242880 | tf_op jit(solution)/shard_map/psum | solution.py:72
  415.3 71.1 %copy-start.2 = (bf16[160,128]{1,0:T(8,128)(2,1)S(1)}, bf16[160,128]{1,0:T(8,128)(2,1)}, u32[]{:S(2)}) copy-start(bf16[160,128]{1,0:T(8,128)(2,1)} %param.5) | copy-start | bytes 122884
  415.4 80.4 %copy-start.1 = (bf16[128,8192]{1,0:T(8,128)(2,1)S(1)}, bf16[128,8192]{1,0:T(8,128)(2,1)}, u32[]{:S(2)}) copy-start(bf16[128,8192]{1,0:T(8,128)(2,1)} %param.6) | copy-start | bytes 6291460
Sparse Core Ops, SparseCore 0:
  415.5 70.9 all-reduce.3
where the time goes:
time: 505 us; the launch traced here: 503 us
  other arithmetic  140 us (28%)
  waiting for transfers between devices  133 us (26%)
  blocking collectives  111 us (22%)
  matrix products  50.1 us (10%)
  local copies, waits for them, and re-layouts  44 us (9%)
  between operations  14.2 us (3%)
  starting transfers between devices  10 us (2%)
    psum x1, blocking collectives, on_device(): summed_pre = lax.psum(partial_pre, 'label')  111 us
    scatter-add x1, other arithmetic, on_device(): jax.ops.segment_sum(back_rows, slot_position.reshape(-1), num_segments=fe...  87.4 us
    psum x1, waiting for transfers between devices, on_device(): lax.psum(column_sum.astype(jnp.bfloat16), 'label').astype(jnp.float32)  56.8 us
    all_to_all x1, waiting for transfers between devices, on_device(): lax.all_to_all(group_part, 'feat', split_axis=0, concat_axis=0, tiled=True)  43.7 us
    all_to_all x1, waiting for transfers between devices, on_device(): lax.all_to_all(outgoing, 'feat', split_axis=0, concat_axis=0, tiled=True)  32.3 us
    scatter-add x1, other arithmetic, on_device(): jax.ops.segment_sum(returned.astype(jnp.float32).reshape(feat_count * CAP...  22.5 us
    dot_general x1, matrix products, on_device(): jnp.einsum('dle,lsce->lsdc', residual, sparse_weight, preferred_element_t...  15.2 us
    gather x1, local copies, waits for them, and re-layouts, on_device(): jnp.take(incoming.reshape(feat_count * CAP, doc_count, BLK), slot_positio...  14.7 us
  transfers between devices with their start and end apart: 3, of which 3 were waited for; matrix products, arithmetic and copies ran while one was open for 5% of the time, Pallas kernels for 0%

commit v1 on v0

--- a/solution.py
+++ b/solution.py
@@ -8,6 +8,22 @@
 SLOTS = 16
 LBLK_DEV = 24
 CAP = 24
+
+
+def save_keys(a0, axis_name):
+    workers = lax.axis_size(axis_name)
+
+    def finish_matrix(now, vec_out):
+        if vec_out >= workers:
+            return now
+        odd = finish_matrix(
+            now + lax.ppermute(now, axis_name, [(ix, ix ^ vec_out) for ix in range(workers)]),
+            2 * vec_out,
+        )
+        return odd
+
+    r_now = finish_matrix(a0, 1)
+    return r_now
 
 
 def on_device(documents, expand_weight, sparse_weight, feature_lists, positives):
@@ -23,7 +39,7 @@
     partial_pre = jnp.einsum(
         "dk,kbc->bdc", documents, local_weight, preferred_element_type=jnp.float32
     )
-    summed_pre = lax.psum(partial_pre, "label")
+    summed_pre = save_keys(partial_pre, "label")
     hidden = jnp.maximum(summed_pre, 0.0).astype(jnp.bfloat16)
     mine = lax.dynamic_slice_in_dim(feature_lists, group * LBLK_DEV, LBLK_DEV, 0)
 

time: 505 us -> 745 us (1.48)
  waiting for transfers between devices: 133 us -> 472 us
  blocking collectives: 111 us -> 0 us
    ppermute x0 -> x3, waiting for transfers between devices: none -> 337 us  [finish_matrix(): lax.ppermute(now, axis_name, [(ix, ix ^ vec_out) for ix in range(workers)])]
    psum x1 -> x0, blocking collectives: 111 us -> none  [on_device(): summed_pre = lax.psum(partial_pre, 'label')]
  transfers between devices with their start and end apart: 3 -> 6, of which waited for: 3 -> 6; matrix products, arithmetic and copies ran while one was open for 5% -> 4% of each run, Pallas kernels for 0% -> 0%
where the time goes in v1:
time: 745 us; the launch traced here: 743 us
  waiting for transfers between devices  472 us (63%)
  other arithmetic  147 us (20%)
  matrix products  47.7 us (6%)
  local copies, waits for them, and re-layouts  45.6 us (6%)
  starting transfers between devices  16.3 us (2%)
  between operations  14.2 us (2%)
    ppermute x3, waiting for transfers between devices, finish_matrix(): lax.ppermute(now, axis_name, [(ix, ix ^ vec_out) for ix in range(workers)])  337 us
    scatter-add x1, other arithmetic, on_device(): jax.ops.segment_sum(back_rows, slot_position.reshape(-1), num_segments=fe...  87.4 us
    psum x1, waiting for transfers between devices, on_device(): lax.psum(column_sum.astype(jnp.bfloat16), 'label').astype(jnp.float32)  55.8 us
    all_to_all x1, waiting for transfers between devices, on_device(): lax.all_to_all(group_part, 'feat', split_axis=0, concat_axis=0, tiled=True)  43.7 us
    all_to_all x1, waiting for transfers between devices, on_device(): lax.all_to_all(outgoing, 'feat', split_axis=0, concat_axis=0, tiled=True)  35.3 us
    scatter-add x1, other arithmetic, on_device(): jax.ops.segment_sum(returned.astype(jnp.float32).reshape(feat_count * CAP...  22.5 us
    dot_general x1, matrix products, on_device(): jnp.einsum('dle,lsce->lsdc', residual, sparse_weight, preferred_element_t...  15.2 us
  transfers between devices with their start and end apart: 6, of which 6 were waited for; matrix products, arithmetic and copies ran while one was open for 4% of the time, Pallas kernels for 0%

profile of v1, /device:TPU:0, one launch (start us, length us, event | category | flops | bytes accessed | tf_op | source)
XLA Modules:
  0.0 743.0 jit_solution(711692055217231544)
XLA Ops:
  10.9 8.3 %collective-permute-done = f32[64,160,128]{2,1,0:T(8,128)S(1)} collective-permute-done((f32[64,160,128]{2,1,0:T(8,128)S(1)}, f32[64,160,128]{2,1,0:T(8,128)S(1)}, u32[]{:S(2)}, u32[]{:S(2)}) %collective-permute-start) | collective-permute-done | bytes 5242912 | tf_op jit(solution)/shard_map/ppermute | solution.py:20
  23.2 113.3 %collective-permute-done.1 = f32[64,160,128]{2,1,0:T(8,128)S(1)} collective-permute-done((f32[64,160,128]{2,1,0:T(8,128)S(1)}, f32[64,160,128]{2,1,0:T(8,128)S(1)}, u32[]{:S(2)}, u32[]{:S(2)}) %collective-permute-start.1) | collective-permute-done | bytes 5242912 | tf_op jit(solution)/shard_map/ppermute | solution.py:20
  142.6 8.2 %while.1 = (s32[]{:T(128)}, s32[768,16]{0,1:T(8,128)}, s32[4,2]{0,1:T(2,128)S(1)}, s32[4,24,16]{1,2,0:T(8,128)S(1)}, s32[]{:T(128)}) while((s32[]{:T(128)}, s32[768,16]{0,1:T(8,128)}, s32[4,2]{0,1:T(2,128)S(1)}, s32[4,24,16]{1,2,0:T(8,128)S(1)}, s32[]{:T(128)}) %tuple.25), condition=%wide.while_cond, body=%wide.while_body.sunk | while | flops 2 | bytes 9825 | solution.py:47
  152.6 215.3 %collective-permute-done.2 = f32[64,160,128]{2,1,0:T(8,128)} collective-permute-done((f32[64,160,128]{2,1,0:T(8,128)}, f32[64,160,128]{2,1,0:T(8,128)}, u32[]{:S(2)}, u32[]{:S(2)}) %collective-permute-start.2) | collective-permute-done | bytes 5242912 | tf_op jit(solution)/shard_map/ppermute | solution.py:20
  367.9 6.6 maximum_convert_fusion
  374.4 4.8 gather_fusion.1
  379.3 4.5 broadcast_select_fusion.5
  383.7 5.0 all-to-all-start
  397.4 35.3 %all-to-all-done = bf16[4,24,160,128]{3,2,1,0:T(8,128)(2,1)} async-done(((bf16[4,24,160,128]{3,2,1,0:T(8,128)(2,1)}), bf16[4,24,160,128]{3,2,1,0:T(8,128)(2,1)}, u32[]{:S(2)}, u32[]{:S(2)}) %all-to-all-start) | async-done | bytes 3932192 | tf_op jit(solution)/shard_map/all_to_all | solution.py:57
  432.7 14.7 %gather_fusion.2 = bf16[384,160,128]{2,1,0:T(8,128)(2,1)} fusion(bf16[96,160,128]{2,1,0:T(8,128)(2,1)} %bitcast.3, s32[1024]{0:T(1024)S(1)} %pad_clamp_fusion), kind=kCustom, calls=%fused_computation.2 | custom fusion | bytes 31458816 | tf_op jit(solution)/shard_map/jit(_take)/gather | solution.py:64
  447.4 11.4 %fusion.14 = bf16[160,24,128,1]{2,0,3,1:T(8,128)(2,1)S(1)} fusion(pred[160,24,128]{2,1,0:T(8,128)(4,1)S(1)} %compare_reduce_fusion, bf16[24,16,128,128]{3,2,1,0:T(8,128)(2,1)} %param.7, bf16[24,16,160,128]{3,2,1,0:T(8,128)(2,1)} %bitcast.62, pred[24,16]{1,0:T(8,128)(4,1)S(1)} %get-tuple-element.26), kind=kOutput, calls=%fused_computation.30 | convolution fusion | flops 2024079360 | bytes 29786496 | tf_op jit(solution)/shard_map/lsdc,lsce->dle/dot_general | solution.py:65
  458.9 15.2 %fusion.23 = f32[24,160,16,128]{3,1,2,0:T(8,128)} fusion(bf16[160,24,128,1]{2,0,3,1:T(8,128)(2,1)S(1)} %fusion.14, bf16[24,16,128,128]{3,2,1,0:T(8,128)(2,1)} %param.7), kind=kOutput, calls=%fused_computation.58 | convolution fusion | flops 2013265920 | bytes 45023232 | tf_op jit(solution)/shard_map/dle,lsce->lsdc/dot_general | solution.py:76
  474.1 4.2 broadcast_in_dim.58
  478.3 87.4 %scatter_fusion = f32[96,160,128]{2,1,0:T(8,128)} fusion(f32[96,160,128]{2,1,0:T(8,128)} %broadcast_in_dim.58, s32[384]{0:T(512)S(1)} %reshape.186, f32[384,160,128]{2,1,0:T(8,128)} %bitcast.61), kind=kCustom, calls=%fused_computation.3 | custom fusion | flops 7864320 | bytes 94373376 | tf_op jit(solution)/shard_map/scatter-add | solution.py:78
  565.7 5.8 convert_element_type.45
  571.6 4.8 all-to-all-start.1
  576.8 43.7 %all-to-all-done.1 = bf16[4,24,160,128]{3,2,1,0:T(8,128)(2,1)} async-done(((bf16[4,24,160,128]{3,2,1,0:T(8,128)(2,1)}), bf16[4,24,160,128]{3,2,1,0:T(8,128)(2,1)}, u32[]{:S(2)}, u32[]{:S(2)}) %all-to-all-start.1) | async-done | bytes 3932192 | tf_op jit(solution)/shard_map/all_to_all | solution.py:82
  620.5 6.4 bitcast_convert_fusion
  629.9 22.5 %scatter_fusion.1 = f32[64,160,128]{2,1,0:T(8,128)} fusion(f32[64,160,128]{2,1,0:T(8,128)} %broadcast.134, s32[96]{0:T(128)S(1)} %reshape.194, f32[96,160,128]{2,1,0:T(8,128)} %bitcast_convert_fusion), kind=kCustom, calls=%fused_computation.4 | custom fusion | flops 1966080 | bytes 23593344 | tf_op jit(solution)/shard_map/scatter-add | solution.py:83
  652.4 4.4 convert_element_type.46
  656.8 14.3 %fusion.4 = bf16[24,16,128,128]{3,2,1,0:T(8,128)(2,1)} fusion(bf16[160,24,128,1]{2,0,3,1:T(8,128)(2,1)S(1)} %fusion.14, bf16[24,16,160,128]{3,2,1,0:T(8,128)(2,1)} %bitcast.63, pred[24,16]{1,0:T(8,128)(4,1)S(1)} %get-tuple-element.26), kind=kOutput, calls=%fused_computation.13 | convolution fusion | flops 2027421696 | bytes 29294976 | tf_op jit(solution)/shard_map/lsdc,dle->lsce/dot_general | solution.py:73
  671.1 55.8 %all-reduce.3.cloned.1.call-done = bf16[64,160,128]{2,1,0:T(8,128)(2,1)} async-done(((bf16[64,160,128]{2,1,0:T(8,128)(2,1)}), bf16[64,160,128]{2,1,0:T(8,128)(2,1)}) %all-reduce.3.cloned.1.call-update) | async-done | bytes 2621456 | tf_op jit(solution)/shard_map/psum | solution.py:88
  726.9 5.2 fusion.13
  732.0 4.1 copy.28
  (72 shorter events, 35.8 us)
Async XLA Ops:
  7.2 1.6 copy-start
  10.4 8.8 %collective-permute-start = (f32[64,160,128]{2,1,0:T(8,128)S(1)}, f32[64,160,128]{2,1,0:T(8,128)S(1)}, u32[]{:S(2)}, u32[]{:S(2)}) collective-permute-start(f32[64,160,128]{2,1,0:T(8,128)S(1)} %convolution_bitcast_fusion), channel_id=1, source_target_pairs={{0,1},{1,0},{2,3},{3,2},{4,5},{5,4},{6,7},{7,6},{8,9},{9,8},{10,11... | collective-permute-start | bytes 15728648 | tf_op jit(solution)/shard_map/ppermute | solution.py:20
  20.2 116.3 %collective-permute-start.1 = (f32[64,160,128]{2,1,0:T(8,128)S(1)}, f32[64,160,128]{2,1,0:T(8,128)S(1)}, u32[]{:S(2)}, u32[]{:S(2)}) collective-permute-start(f32[64,160,128]{2,1,0:T(8,128)S(1)} %add.130), channel_id=1, source_target_pairs={{0,2},{1,3},{2,0},{3,1},{4,6},{5,7},{6,4},{7,5},{8,10},{9,11},{10,... | collective-permute-start | bytes 15728648 | tf_op jit(solution)/shard_map/ppermute | solution.py:20
  139.8 228.1 %collective-permute-start.2 = (f32[64,160,128]{2,1,0:T(8,128)}, f32[64,160,128]{2,1,0:T(8,128)}, u32[]{:S(2)}, u32[]{:S(2)}) collective-permute-start(f32[64,160,128]{2,1,0:T(8,128)} %add.131), channel_id=1, source_target_pairs={{0,4},{1,5},{2,6},{3,7},{4,0},{5,1},{6,2},{7,3},{8,12},{9,13},{10,... | collective-permute-start | bytes 15728648 | tf_op jit(solution)/shard_map/ppermute | solution.py:20
  383.7 49.0 %all-to-all-start = ((bf16[4,24,160,128]{3,2,1,0:T(8,128)(2,1)}), bf16[4,24,160,128]{3,2,1,0:T(8,128)(2,1)}, u32[]{:S(2)}, u32[]{:S(2)}) async-start(bf16[4,24,160,128]{3,2,1,0:T(8,128)(2,1)} %broadcast_select_fusion.5), calls=%async_computation | async-start | bytes 7864320 | tf_op jit(solution)/shard_map/all_to_all | solution.py:57
  390.4 3.1 copy-start.3
  571.6 48.9 %all-to-all-start.1 = ((bf16[4,24,160,128]{3,2,1,0:T(8,128)(2,1)}), bf16[4,24,160,128]{3,2,1,0:T(8,128)(2,1)}, u32[]{:S(2)}, u32[]{:S(2)}) async-start(bf16[4,24,160,128]{3,2,1,0:T(8,128)(2,1)} %bitcast.64), calls=%async_computation.1 | async-start | bytes 7864320 | tf_op jit(solution)/shard_map/all_to_all | solution.py:82
  576.4 150.5 %all-reduce.3.cloned.1.call-start = ((), (), s32[]{:S(2)}) async-start(), calls=%async_computation.2 | async-start | bytes 5242880 | tf_op jit(solution)/shard_map/psum | solution.py:88
  656.8 70.1 %copy-start.2 = (bf16[160,128]{1,0:T(8,128)(2,1)S(1)}, bf16[160,128]{1,0:T(8,128)(2,1)}, u32[]{:S(2)}) copy-start(bf16[160,128]{1,0:T(8,128)(2,1)} %param.5) | copy-start | bytes 122884
  656.8 79.3 %copy-start.1 = (bf16[128,8192]{1,0:T(8,128)(2,1)S(1)}, bf16[128,8192]{1,0:T(8,128)(2,1)}, u32[]{:S(2)}) copy-start(bf16[128,8192]{1,0:T(8,128)(2,1)} %param.6) | copy-start | bytes 6291460
Sparse Core Ops, SparseCore 0:
  656.9 69.8 all-reduce.2
